TPU v7x, 32 devices: a whole 2x2x4 slice. The times are simulated.
32 devices in a mesh: row: 2 (over y), col: 16 (over z, x, core).
Axes of the slice: x: 2, y: 2, z: 4, core: 2. Of those that a mesh axis runs over, the one named last changes fastest.
Arguments:
- tokens: bfloat16 [16384, 1152], P(('col', 'row')), may hold values from -6 to 6
- labels: int32 [64], P('col'), may hold values from 0 to 999
- timesteps: int32 [64], P('col'), may hold values from 0 to 999
- class_table: bfloat16 [1000, 1152], replicated, may hold values from -6 to 6
- ada_weight: bfloat16 [1152, 6912], P('col', 'row'), may hold values from -0.1875 to 0.1875
- ada_bias: bfloat16 [6912], P(('row', 'col')), may hold values from -3 to 3
- qkv_weight: bfloat16 [3, 1152, 1152], P(None, 'col', 'row'), may hold values from -0.1875 to 0.1875
- qkv_bias: bfloat16 [2304], P(('row', 'col')), may hold values from -3 to 3
- proj_weight: bfloat16 [1152, 1152], P('row', 'col'), may hold values from -0.75 to 0.75
- proj_bias: bfloat16 [1152], P('col'), may hold values from -3 to 3
- up_weight: bfloat16 [1152, 4608], P('col', 'row'), may hold values from -0.1875 to 0.1875
- up_bias: bfloat16 [4608], P(('row', 'col')), may hold values from -3 to 3
- down_weight: bfloat16 [4608, 1152], P('row', 'col'), may hold values from -0.09375 to 0.09375
- down_bias: bfloat16 [1152], P('col'), may hold values from -3 to 3
- cotangent: bfloat16 [16384, 1152], P(('col', 'row')), may hold values from -6 to 6
Outputs:
- block_out: bfloat16 [16384, 1152], P(('col', 'row'))
- tokens_grad: float32 [16384, 1152], P(('col', 'row'))
- cond_grad: float32 [64, 1152], P('col', 'row')
- ada_weight_grad: float32 [1152, 6912], P('col', 'row')
- ada_bias_grad: float32 [6912], P(('row', 'col'))
- qkv_weight_grad: float32 [3, 1152, 1152], P(None, 'col', 'row')
- qkv_bias_grad: float32 [2304], P(('row', 'col'))
- proj_weight_grad: float32 [1152, 1152], P('row', 'col')
- proj_bias_grad: float32 [1152], P('col')
- up_weight_grad: float32 [1152, 4608], P('col', 'row')
- up_bias_grad: float32 [4608], P(('row', 'col'))
- down_weight_grad: float32 [4608, 1152], P('row', 'col')
- down_bias_grad: float32 [1152], P('col')
All inputs are finite; a program needn't handle non-finite values.
Results may differ from a plain program's by a relative error of at most 0.02.
Values may be sent and summed in bfloat16 or wider, within the bound.
A program may use at most 256 MiB of HBM per device.

v0:
```python
import math

import jax
import jax.numpy as jnp
from jax import lax
from jax.sharding import PartitionSpec as P

D = 1152
HD = 72
SEQ = 256


EPS = 1e-06
GELU_K = math.sqrt(2.0 / math.pi)
GELU_C = 0.044715


def condition(labels, timesteps, class_table):
    classes = jnp.arange(class_table.shape[0], dtype=jnp.int32)
    onehot = (labels[:, None] == classes[None, :]).astype(jnp.bfloat16)
    embedded = jnp.dot(onehot, class_table, preferred_element_type=jnp.float32)
    half_width = class_table.shape[1] // 2
    frequencies = jnp.exp(
        -math.log(10000.0) * jnp.arange(half_width, dtype=jnp.float32) / half_width
    )
    angles = timesteps.astype(jnp.float32)[:, None] * frequencies[None, :]
    return embedded + jnp.concatenate([jnp.cos(angles), jnp.sin(angles)], axis=1)


def normalize(values):
    row_mean = jnp.mean(values, axis=-1, keepdims=True)
    centred = values - row_mean
    inv_std = lax.rsqrt(jnp.mean(centred * centred, axis=-1, keepdims=True) + EPS)
    return (centred * inv_std, inv_std)


def normalize_back(normed, inv_std, upstream):
    return inv_std * (
        upstream
        - jnp.mean(upstream, axis=-1, keepdims=True)
        - normed * jnp.mean(upstream * normed, axis=-1, keepdims=True)
    )


def gelu_pair(inputs):
    tanh_part = jnp.tanh(GELU_K * (inputs + GELU_C * inputs * inputs * inputs))
    values = 0.5 * inputs * (1.0 + tanh_part)
    slopes = 0.5 * (1.0 + tanh_part) + 0.5 * inputs * (1.0 - tanh_part * tanh_part) * GELU_K * (
        1.0 + 3.0 * GELU_C * inputs * inputs
    )
    return (values, slopes)


def contract_rows(left, right):
    return lax.dot_general(
        left, right, (((0,), (0,)), ((), ())), preferred_element_type=jnp.float32
    )


def contract_cols(left, right):
    return lax.dot_general(
        left, right, (((1,), (1,)), ((), ())), preferred_element_type=jnp.float32
    )


def contract_cross(left, right):
    return lax.dot_general(
        left, right, (((0,), (1,)), ((), ())), preferred_element_type=jnp.float32
    )


def exact_rows(left, right):
    return lax.dot_general(
        left,
        right,
        (((0,), (0,)), ((), ())),
        precision=lax.Precision.HIGHEST,
        preferred_element_type=jnp.float32,
    )


def attend(query_cols, key_cols, value_cols, heads, latents):
    head_shape = (heads, HD, latents, SEQ)
    inv_root = 1.0 / math.sqrt(HD)
    query_heads = query_cols.reshape(head_shape)
    key_heads = key_cols.reshape(head_shape)
    value_heads = value_cols.reshape(head_shape)
    scores = (
        jnp.einsum("hels,helt->lhst", query_heads, key_heads, preferred_element_type=jnp.float32)
        * inv_root
    )
    top_score = jnp.max(scores, axis=-1, keepdims=True)
    unnormed = jnp.exp(scores - top_score)
    totals = jnp.sum(unnormed, axis=-1, keepdims=True)
    logsum = top_score + jnp.log(totals)
    attn_probs = (unnormed / totals).astype(jnp.bfloat16)
    attended = jnp.einsum(
        "lhst,helt->hels", attn_probs, value_heads, preferred_element_type=jnp.float32
    ).astype(jnp.bfloat16)
    return (attended.reshape(query_cols.shape), logsum)


def attend_back(query_cols, key_cols, value_cols, logsum, upstream_cols, heads, latents):
    head_shape = (heads, HD, latents, SEQ)
    inv_root = 1.0 / math.sqrt(HD)
    query_heads = query_cols.reshape(head_shape)
    key_heads = key_cols.reshape(head_shape)
    value_heads = value_cols.reshape(head_shape)
    upstream_heads = upstream_cols.reshape(head_shape)
    scores = (
        jnp.einsum("hels,helt->lhst", query_heads, key_heads, preferred_element_type=jnp.float32)
        * inv_root
    )
    attn_probs = jnp.exp(scores - logsum)
    probs_low = attn_probs.astype(jnp.bfloat16)
    grad_values = jnp.einsum(
        "lhst,hels->helt", probs_low, upstream_heads, preferred_element_type=jnp.float32
    ).astype(jnp.bfloat16)
    grad_probs = jnp.einsum(
        "hels,helt->lhst", upstream_heads, value_heads, preferred_element_type=jnp.float32
    )
    row_inner = jnp.sum(attn_probs * grad_probs, axis=-1, keepdims=True)
    grad_scores = (attn_probs * (grad_probs - row_inner) * inv_root).astype(jnp.bfloat16)
    grad_query = jnp.einsum(
        "lhst,helt->hels", grad_scores, key_heads, preferred_element_type=jnp.float32
    ).astype(jnp.bfloat16)
    grad_keys = jnp.einsum(
        "lhst,hels->helt", grad_scores, query_heads, preferred_element_type=jnp.float32
    ).astype(jnp.bfloat16)
    return (
        grad_query.reshape(query_cols.shape),
        grad_keys.reshape(query_cols.shape),
        grad_values.reshape(query_cols.shape),
    )


def local(
    tokens,
    labels,
    timesteps,
    class_table,
    ada_weight,
    ada_bias,
    qkv_weight,
    qkv_bias,
    proj_weight,
    proj_bias,
    up_weight,
    up_bias,
    down_weight,
    down_bias,
    cotangent,
):
    local_rows = tokens.shape[0]
    latents = labels.shape[0]
    row_devices = lax.axis_size("row")
    gathered = (
        lax.all_gather(ada_weight, "col", axis=0, tiled=True),
        lax.all_gather(ada_bias, "col", axis=0, tiled=True),
        lax.all_gather(qkv_weight, "col", axis=1, tiled=True),
        lax.all_gather(qkv_bias, "col", axis=0, tiled=True),
        lax.all_gather(proj_weight, "col", axis=1, tiled=True),
        lax.all_gather(proj_bias, "col", axis=0, tiled=True),
        lax.all_gather(up_weight, "col", axis=0, tiled=True),
        lax.all_gather(up_bias, "col", axis=0, tiled=True),
        lax.all_gather(down_weight, "col", axis=1, tiled=True),
        lax.all_gather(down_bias, "col", axis=0, tiled=True),
    )
    (
        ada_full,
        ada_bias_full,
        qkv_full,
        qkv_bias_full,
        proj_full,
        proj_bias_full,
        up_full,
        up_bias_full,
        down_full,
        down_bias_full,
    ) = gathered
    local_width = qkv_full.shape[2]
    local_heads = local_width // HD
    row_latent = (
        lax.axis_index("row") * local_rows + jnp.arange(local_rows, dtype=jnp.int32)
    ) // SEQ
    picker = (row_latent[:, None] == jnp.arange(latents, dtype=jnp.int32)[None, :]).astype(
        jnp.float32
    )
    conditioning = condition(labels, timesteps, class_table)
    sigmoid_cond = jax.nn.sigmoid(conditioning)
    activated = (conditioning * sigmoid_cond).astype(jnp.bfloat16)
    partial_mod = jnp.dot(
        activated, ada_full, preferred_element_type=jnp.float32
    ) + ada_bias_full.astype(jnp.float32)
    modulation = lax.all_gather(partial_mod, "row", axis=1, tiled=True)
    mod_rows = jnp.dot(
        picker, modulation, precision=lax.Precision.HIGHEST, preferred_element_type=jnp.float32
    )
    parts = [mod_rows[:, block * D : (block + 1) * D] for block in range(6)]
    shift_one, scale_one, gate_one, shift_two, scale_two, gate_two = parts
    source = tokens.astype(jnp.float32)
    normed_one, inv_one = normalize(source)
    hidden_one = (normed_one * (1.0 + scale_one) + shift_one).astype(jnp.bfloat16)
    flat_one = lax.all_gather(hidden_one, "row", axis=0, tiled=True)
    bias_pair = qkv_bias_full.astype(jnp.float32).reshape(local_heads, 2, HD)
    query_bias = bias_pair[:, 0].reshape(local_width, 1)
    value_bias = bias_pair[:, 1].reshape(local_width, 1)
    query_cols = (contract_cross(qkv_full[0], flat_one) + query_bias).astype(jnp.bfloat16)
    key_cols = contract_cross(qkv_full[1], flat_one).astype(jnp.bfloat16)
    value_cols = (contract_cross(qkv_full[2], flat_one) + value_bias).astype(jnp.bfloat16)
    attended, logsum = attend(query_cols, key_cols, value_cols, local_heads, latents)
    piece = attended
    attn_out = lax.psum_scatter(
        contract_rows(piece, proj_full).astype(jnp.bfloat16), "row", scatter_dimension=0, tiled=True
    ).astype(jnp.float32) + proj_bias_full.astype(jnp.float32)
    middle = source + gate_one * attn_out
    normed_two, inv_two = normalize(middle)
    hidden_two = (normed_two * (1.0 + scale_two) + shift_two).astype(jnp.bfloat16)
    flat_two = lax.all_gather(hidden_two, "row", axis=0, tiled=True)
    pre_act = jnp.dot(flat_two, up_full, preferred_element_type=jnp.float32) + up_bias_full.astype(
        jnp.float32
    )
    activ_full, slopes = gelu_pair(pre_act)
    activ = activ_full.astype(jnp.bfloat16)
    piece = activ
    mlp_out = lax.psum_scatter(
        jnp.dot(piece, down_full, preferred_element_type=jnp.float32).astype(jnp.bfloat16),
        "row",
        scatter_dimension=0,
        tiled=True,
    ).astype(jnp.float32) + down_bias_full.astype(jnp.float32)
    block_out = (middle + gate_two * mlp_out).astype(jnp.bfloat16)
    upstream = cotangent.astype(jnp.float32)
    grad_mlp = (gate_two * upstream).astype(jnp.bfloat16)
    flat_mlp = lax.all_gather(grad_mlp, "row", axis=0, tiled=True)
    down_weight_grad = contract_rows(activ, flat_mlp)
    down_bias_grad = jnp.sum(flat_mlp, axis=0, dtype=jnp.float32)
    grad_pre = (contract_cols(flat_mlp, down_full) * slopes).astype(jnp.bfloat16)
    up_weight_grad = contract_rows(flat_two, grad_pre)
    up_bias_grad = jnp.sum(grad_pre, axis=0, dtype=jnp.float32)
    piece = grad_pre
    grad_hidden_two = lax.psum_scatter(
        contract_cols(piece, up_full).astype(jnp.bfloat16), "row", scatter_dimension=0, tiled=True
    ).astype(jnp.float32)
    grad_middle = upstream + normalize_back(
        normed_two, inv_two, grad_hidden_two * (1.0 + scale_two)
    )
    grad_attn = (gate_one * grad_middle).astype(jnp.bfloat16)
    flat_grad_attn = lax.all_gather(grad_attn, "row", axis=0, tiled=True)
    proj_weight_grad = jnp.dot(attended, flat_grad_attn, preferred_element_type=jnp.float32)
    proj_bias_grad = jnp.sum(flat_grad_attn, axis=0, dtype=jnp.float32)
    grad_attended = contract_cols(proj_full, flat_grad_attn).astype(jnp.bfloat16)
    grad_query, grad_keys, grad_values = attend_back(
        query_cols, key_cols, value_cols, logsum, grad_attended, local_heads, latents
    )
    qkv_weight_grad = jnp.stack(
        [
            contract_cross(flat_one, grad_query),
            contract_cross(flat_one, grad_keys),
            contract_cross(flat_one, grad_values),
        ],
        axis=0,
    )
    query_sum = jnp.sum(grad_query, axis=1, dtype=jnp.float32)
    value_sum = jnp.sum(grad_values, axis=1, dtype=jnp.float32)
    qkv_bias_grad = jnp.stack(
        [query_sum.reshape(local_heads, HD), value_sum.reshape(local_heads, HD)], axis=1
    ).reshape(2 * local_width)
    total = jnp.zeros((local_rows * lax.axis_size("row"), D), jnp.float32)
    for which, grads in enumerate((grad_query, grad_keys, grad_values)):
        piece = grads
        total = total + contract_cross(piece, qkv_full[which])
    grad_hidden_one = lax.psum_scatter(
        total.astype(jnp.bfloat16), "row", scatter_dimension=0, tiled=True
    ).astype(jnp.float32)
    tokens_grad = grad_middle + normalize_back(
        normed_one, inv_one, grad_hidden_one * (1.0 + scale_one)
    )
    row_terms = jnp.concatenate(
        [
            grad_hidden_one,
            grad_hidden_one * normed_one,
            grad_middle * attn_out,
            grad_hidden_two,
            grad_hidden_two * normed_two,
            upstream * mlp_out,
        ],
        axis=1,
    )
    grad_mod_part = exact_rows(picker, row_terms)
    grad_modulation = lax.psum_scatter(
        grad_mod_part.astype(jnp.bfloat16), "row", scatter_dimension=1, tiled=True
    ).astype(jnp.float32)
    ada_bias_grad = jnp.sum(grad_modulation, axis=0)
    grad_mod_low = grad_modulation.astype(jnp.bfloat16)
    ada_weight_grad = contract_rows(activated, grad_mod_low)
    grad_act_part = contract_cols(grad_mod_low, ada_full)
    grad_activated = lax.psum_scatter(grad_act_part, "row", scatter_dimension=1, tiled=True)
    slice_width = D // row_devices
    cond_slice = lax.dynamic_slice_in_dim(
        conditioning, lax.axis_index("row") * slice_width, slice_width, 1
    )
    sigmoid_slice = jax.nn.sigmoid(cond_slice)
    cond_grad = grad_activated * sigmoid_slice * (1.0 + cond_slice * (1.0 - sigmoid_slice))
    summed_grads = tuple(
        (
            lax.psum_scatter(
                ada_weight_grad.astype(jnp.bfloat16), "col", scatter_dimension=0, tiled=True
            ).astype(jnp.float32),
            lax.psum_scatter(
                ada_bias_grad.astype(jnp.bfloat16), "col", scatter_dimension=0, tiled=True
            ).astype(jnp.float32),
            lax.psum_scatter(
                qkv_weight_grad.astype(jnp.bfloat16), "col", scatter_dimension=1, tiled=True
            ).astype(jnp.float32),
            lax.psum_scatter(
                qkv_bias_grad.astype(jnp.bfloat16), "col", scatter_dimension=0, tiled=True
            ).astype(jnp.float32),
            lax.psum_scatter(
                proj_weight_grad.astype(jnp.bfloat16), "col", scatter_dimension=1, tiled=True
            ).astype(jnp.float32),
            lax.psum_scatter(
                proj_bias_grad.astype(jnp.bfloat16), "col", scatter_dimension=0, tiled=True
            ).astype(jnp.float32),
            lax.psum_scatter(
                up_weight_grad.astype(jnp.bfloat16), "col", scatter_dimension=0, tiled=True
            ).astype(jnp.float32),
            lax.psum_scatter(
                up_bias_grad.astype(jnp.bfloat16), "col", scatter_dimension=0, tiled=True
            ).astype(jnp.float32),
            lax.psum_scatter(
                down_weight_grad.astype(jnp.bfloat16), "col", scatter_dimension=1, tiled=True
            ).astype(jnp.float32),
            lax.psum_scatter(
                down_bias_grad.astype(jnp.bfloat16), "col", scatter_dimension=0, tiled=True
            ).astype(jnp.float32),
        )
    )
    return (block_out, tokens_grad, cond_grad) + summed_grads


def solution(mesh):
    in_specs = (
        P(("col", "row"), None),
        P("col"),
        P("col"),
        P(),
        P("col", "row"),
        P(("row", "col")),
        P(None, "col", "row"),
        P(("row", "col")),
        P("row", "col"),
        P("col"),
        P("col", "row"),
        P(("row", "col")),
        P("row", "col"),
        P("col"),
        P(("col", "row"), None),
    )
    out_specs = (
        P(("col", "row"), None),
        P(("col", "row"), None),
        P("col", "row"),
        P("col", "row"),
        P(("row", "col")),
        P(None, "col", "row"),
        P(("row", "col")),
        P("row", "col"),
        P("col"),
        P("col", "row"),
        P(("row", "col")),
        P("row", "col"),
        P("col"),
    )
    return jax.shard_map(local, mesh=mesh, in_specs=in_specs, out_specs=out_specs, check_vma=False)
```

profile of v0, /device:TPU:0, one launch (start us, length us, event | category | flops | bytes accessed | tf_op | source)
XLA Modules:
  0.0 1198.5 jit_solution(12560479045379927398)
XLA Ops:
  17.4 66.0 %all-reduce.14 = (bf16[1152]{0:T(1024)(128)(2,1)S(1)}, bf16[3456]{0:T(1024)(128)(2,1)S(1)}, bf16[1152]{0:T(1024)(128)(2,1)S(1)}, bf16[2304]{0:T(1024)(128)(2,1)S(1)}, bf16[1152]{0:T(1024)(128)(2,1)S(1)}) all-reduce(bf16[1152]{0:T(1024)(128)(2,1)S(1)} %dynamic-update-slice.1, ...), channel_id=1, replica_groups=mesh['row'=2,'col'=16] {'col'}, use_global_device_ids=true, to_apply=%add.1 | all-reduce | flops 9216 | bytes 36864
  109.2 28.8 %all-gather.14.cloned.1.call-done = bf16[3,1152,576]{2,1,0:T(8,128)(2,1)} async-done(((bf16[3,72,576]{2,1,0:T(8,128)(2,1)}), bf16[3,1152,576]{2,1,0:T(8,128)(2,1)}) %all-gather.14.cloned.1.call-update) | async-done | bytes 3981328 | tf_op jit(solution)/shard_map/all_gather | solution.py:160
  137.9 36.7 %all-gather.12.cloned.1.call-done = bf16[1024,1152]{1,0:T(8,128)(2,1)} async-done(((bf16[512,1152]{1,0:T(8,128)(2,1)}), bf16[1024,1152]{1,0:T(8,128)(2,1)}) %all-gather.12.cloned.1.call-update) | async-done | bytes 2359312 | tf_op jit(solution)/shard_map/all_gather | solution.py:204
  221.8 33.1 %reduce-scatter.19.cloned.1.call-done = bf16[512,1152]{1,0:T(8,128)(2,1)} async-done(((bf16[1024,1152]{1,0:T(8,128)(2,1)}), bf16[512,1152]{1,0:T(8,128)(2,1)}) %reduce-scatter.19.cloned.1.call-update) | async-done | bytes 1179664 | tf_op jit(solution)/shard_map/reduce_scatter | solution.py:213
  266.3 47.0 %all-gather.20.cloned.1.call-done = bf16[1152,2304]{1,0:T(8,128)(2,1)} async-done(((bf16[72,2304]{1,0:T(8,128)(2,1)}), bf16[1152,2304]{1,0:T(8,128)(2,1)}) %all-gather.20.cloned.1.call-update) | async-done | bytes 5308432 | tf_op jit(solution)/shard_map/all_gather | solution.py:164
  313.3 36.8 %all-gather.18.cloned.1.call-done = bf16[1024,1152]{1,0:T(8,128)(2,1)} async-done(((bf16[512,1152]{1,0:T(8,128)(2,1)}), bf16[1024,1152]{1,0:T(8,128)(2,1)}) %all-gather.18.cloned.1.call-update) | async-done | bytes 2359312 | tf_op jit(solution)/shard_map/all_gather | solution.py:219
  350.1 11.5 fusion.103
  361.7 47.0 %all-gather.22.cloned.1.call-done = bf16[2304,1152]{0,1:T(8,128)(2,1)} async-done(((bf16[2304,72]{0,1:T(8,128)(2,1)}), bf16[2304,1152]{0,1:T(8,128)(2,1)}) %all-gather.22.cloned.1.call-update) | async-done | bytes 5308432 | tf_op jit(solution)/shard_map/all_gather | solution.py:166
  408.6 36.8 %all-gather.24.cloned.1.call-done = bf16[1024,1152]{1,0:T(8,128)(2,1)} async-done(((bf16[512,1152]{1,0:T(8,128)(2,1)}), bf16[1024,1152]{1,0:T(8,128)(2,1)}) %all-gather.24.cloned.1.call-update) | async-done | bytes 2359312 | tf_op jit(solution)/shard_map/all_gather | solution.py:235
  445.4 14.2 %fusion.102 = (bf16[2304]{0:T(1024)(128)(2,1)S(1)}, bf16[1024,2304]{1,0:T(8,128)(2,1)S(1)}) fusion(f32[1024,2304]{1,0:T(8,128)} %fusion.103, f32[2304]{0:T(1024)S(1)} %convert_element_type.214, bf16[1024,1152]{1,0:T(8,128)(2,1)} %all-gather.24.cloned.1.call-done, bf16[2304,1152]{0,1:T(8,128)(2,1)} %all-gather.22.cloned.1.call-done), kind=kOutput, calls=%fused_computation.169 | convolution fusion | flops 5485361152 | bytes 21837312 | tf_op jit(solution)/shard_map/dot_general | solution.py:61
  472.0 13.9 %convolution_convert_fusion.5 = bf16[1024,1152]{1,0:T(8,128)(2,1)} fusion(bf16[2304,1152]{0,1:T(8,128)(2,1)} %all-gather.22.cloned.1.call-done, f32[1024,2304]{1,0:T(8,128)} %fusion.103, f32[2304]{0:T(1024)S(1)} %convert_element_type.214), kind=kOutput, calls=%fused_computation.34 | convolution fusion | flops 5460590592 | bytes 17114112 | tf_op jit(solution)/shard_map/dot_general | solution.py:227
  486.0 20.9 %reduce-scatter.23.cloned.1.call-done = bf16[512,1152]{1,0:T(8,128)(2,1)} async-done(((bf16[1024,1152]{1,0:T(8,128)(2,1)}), bf16[512,1152]{1,0:T(8,128)(2,1)}) %reduce-scatter.23.cloned.1.call-update) | async-done | bytes 1179664 | tf_op jit(solution)/shard_map/reduce_scatter | solution.py:242
  510.5 33.5 %reduce-scatter.21.cloned.1.call-done = bf16[512,1152]{1,0:T(8,128)(2,1)} async-done(((bf16[1024,1152]{1,0:T(8,128)(2,1)}), bf16[512,1152]{1,0:T(8,128)(2,1)}) %reduce-scatter.21.cloned.1.call-update) | async-done | bytes 1179664 | tf_op jit(solution)/shard_map/reduce_scatter | solution.py:226
  550.6 36.1 %all-gather.26.cloned.1.call-done = bf16[1024,1152]{1,0:T(8,128)(2,1)} async-done(((bf16[512,1152]{1,0:T(8,128)(2,1)}), bf16[1024,1152]{1,0:T(8,128)(2,1)}) %all-gather.26.cloned.1.call-update) | async-done | bytes 2359312 | tf_op jit(solution)/shard_map/all_gather | solution.py:249
  626.4 34.6 %reduce-scatter.25.cloned.1.call-done = bf16[512,1152]{1,0:T(8,128)(2,1)} async-done(((bf16[1024,1152]{1,0:T(8,128)(2,1)}), bf16[512,1152]{1,0:T(8,128)(2,1)}) %reduce-scatter.25.cloned.1.call-update) | async-done | bytes 1179664 | tf_op jit(solution)/shard_map/reduce_scatter | solution.py:273
  679.8 11.6 convolution_convert_fusion.1
  691.9 10.5 convolution_convert_fusion.2
  712.8 11.5 copy.92
  749.5 40.8 %reduce-scatter.29.cloned.1.call-done = bf16[2304,72]{0,1:T(8,128)(2,1)} async-done(((bf16[2304,1152]{0,1:T(8,128)(2,1)}), bf16[2304,72]{0,1:T(8,128)(2,1)}) %reduce-scatter.29.cloned.1.call-update) | async-done | bytes 331792 | tf_op jit(solution)/shard_map/reduce_scatter | solution.py:331
  792.1 79.2 %reduce-scatter.27.cloned.1.call-done = bf16[72,2304]{1,0:T(8,128)(2,1)} async-done(((bf16[1152,2304]{1,0:T(8,128)(2,1)}), bf16[72,2304]{1,0:T(8,128)(2,1)}) %reduce-scatter.27.cloned.1.call-update) | async-done | bytes 331792 | tf_op jit(solution)/shard_map/reduce_scatter | solution.py:325
  873.1 134.5 %all-reduce.17.cloned.1.call-done = bf16[3,1152,576]{2,0,1:T(4,128)(2,1)} async-done(((bf16[3,1152,576]{2,0,1:T(4,128)(2,1)}), bf16[3,1152,576]{2,0,1:T(4,128)(2,1)}) %all-reduce.17.cloned.1.call-update) | async-done | bytes 3981328
  1009.7 59.5 %reduce-scatter.37.cloned.1.call-done = bf16[576,72]{0,1:T(8,128)(2,1)} async-done(((bf16[576,1152]{0,1:T(8,128)(2,1)}), bf16[576,72]{0,1:T(8,128)(2,1)}) %reduce-scatter.37.cloned.1.call-update) | async-done | bytes 82960
  1071.1 58.4 %all-reduce.13 = (bf16[3456]{0:T(1024)(128)(2,1)S(1)}, bf16[1152]{0:T(1024)(128)(2,1)S(1)}, bf16[1152]{0:T(1024)(128)(2,1)S(1)}, bf16[2304]{0:T(1024)(128)(2,1)S(1)}, bf16[1152]{0:T(1024)(128)(2,1)S(1)}) all-reduce(bf16[3456]{0:T(1024)(128)(2,1)S(1)} %bitcast_reduce_fusion, ...), channel_id=9, replica_groups=mesh['row'=2,'col'=16] {'col'}, use_global_device_ids=true, to_apply=%region_19.20.clone | all-reduce | flops 9216 | bytes 36864
  1134.3 55.1 %reduce-scatter.35.cloned.1.call-done = bf16[72,3456]{1,0:T(8,128)(2,1)} async-done(((bf16[1152,3456]{1,0:T(8,128)(2,1)}), bf16[72,3456]{1,0:T(8,128)(2,1)}) %reduce-scatter.35.cloned.1.call-update) | async-done | bytes 497680
  (238 shorter events, 221.4 us)
Async XLA Ops:
  7.2 78.4 %copy-start = (bf16[1000,1152]{1,0:T(8,128)(2,1)S(1)}, bf16[1000,1152]{1,0:T(8,128)(2,1)}, u32[]{:S(2)}) copy-start(bf16[1000,1152]{1,0:T(8,128)(2,1)} %param.18) | copy-start | bytes 6912004
  7.2 77.7 %copy-start.6 = (bf16[512,1152]{1,0:T(8,128)(2,1)S(1)}, bf16[512,1152]{1,0:T(8,128)(2,1)}, u32[]{:S(2)}) copy-start(bf16[512,1152]{1,0:T(8,128)(2,1)} %param.15) | copy-start | bytes 3538948
  7.2 78.9 %all-gather.10.cloned.1.call-start = ((), (), s32[]{:S(2)}) async-start(), calls=%async_computation.10 | async-start | bytes 8460288 | tf_op jit(solution)/shard_map/all_gather | solution.py:158
  7.9 130.0 %all-gather.14.cloned.1.call-start = ((), (), s32[]{:S(2)}) async-start(), calls=%async_computation.12 | async-start | bytes 4700160 | tf_op jit(solution)/shard_map/all_gather | solution.py:160
  8.7 165.9 %all-gather.12.cloned.1.call-start = ((), (), s32[]{:S(2)}) async-start(), calls=%async_computation.11 | async-start | bytes 3538944 | tf_op jit(solution)/shard_map/all_gather | solution.py:204
  107.8 108.0 %all-gather.16.cloned.1.call-start = ((), (), s32[]{:S(2)}) async-start(), calls=%async_computation.13 | async-start | bytes 1566720 | tf_op jit(solution)/shard_map/all_gather | solution.py:162
  108.4 146.6 %reduce-scatter.19.cloned.1.call-start = ((), (), s32[]{:S(2)}) async-start(), calls=%async_computation.14 | async-start | bytes 3538944 | tf_op jit(solution)/shard_map/reduce_scatter | solution.py:213
  221.2 92.1 %all-gather.20.cloned.1.call-start = ((), (), s32[]{:S(2)}) async-start(), calls=%async_computation.16 | async-start | bytes 5640192 | tf_op jit(solution)/shard_map/all_gather | solution.py:164
  221.8 128.4 %all-gather.18.cloned.1.call-start = ((), (), s32[]{:S(2)}) async-start(), calls=%async_computation.15 | async-start | bytes 3538944 | tf_op jit(solution)/shard_map/all_gather | solution.py:219
  264.7 143.9 %all-gather.22.cloned.1.call-start = ((), (), s32[]{:S(2)}) async-start(), calls=%async_computation.17 | async-start | bytes 5640192 | tf_op jit(solution)/shard_map/all_gather | solution.py:166
  265.5 179.9 %all-gather.24.cloned.1.call-start = ((), (), s32[]{:S(2)}) async-start(), calls=%async_computation.19 | async-start | bytes 3538944 | tf_op jit(solution)/shard_map/all_gather | solution.py:235
  266.2 240.6 %reduce-scatter.23.cloned.1.call-start = ((), (), s32[]{:S(2)}) async-start(), calls=%async_computation.20 | async-start | bytes 3538944 | tf_op jit(solution)/shard_map/reduce_scatter | solution.py:242
  471.9 72.0 %reduce-scatter.21.cloned.1.call-start = ((), (), s32[]{:S(2)}) async-start(), calls=%async_computation.18 | async-start | bytes 3538944 | tf_op jit(solution)/shard_map/reduce_scatter | solution.py:226
  485.9 100.8 %all-gather.26.cloned.1.call-start = ((), (), s32[]{:S(2)}) async-start(), calls=%async_computation.21 | async-start | bytes 3538944 | tf_op jit(solution)/shard_map/all_gather | solution.py:249
  506.9 37.1 %copy-start.7 = (bf16[512,1152]{1,0:T(8,128)(2,1)S(1)}, bf16[512,1152]{1,0:T(8,128)(2,1)}, u32[]{:S(2)}) copy-start(bf16[512,1152]{1,0:T(8,128)(2,1)} %reduce-scatter.23.cloned.1.call-done) | copy-start | bytes 3538948
  550.5 110.5 %reduce-scatter.25.cloned.1.call-start = ((), (), s32[]{:S(2)}) async-start(), calls=%async_computation.22 | async-start | bytes 3538944 | tf_op jit(solution)/shard_map/reduce_scatter | solution.py:273
  626.2 104.7 %reduce-scatter.31.cloned.1.call-start = ((), (), s32[]{:S(2)}) async-start(), calls=%async_computation.25 | async-start | bytes 2654208
  679.8 110.4 %reduce-scatter.29.cloned.1.call-start = ((), (), s32[]{:S(2)}) async-start(), calls=%async_computation.24 | async-start | bytes 5640192 | tf_op jit(solution)/shard_map/reduce_scatter | solution.py:331
  691.4 179.8 %reduce-scatter.27.cloned.1.call-start = ((), (), s32[]{:S(2)}) async-start(), calls=%async_computation.23 | async-start | bytes 5640192 | tf_op jit(solution)/shard_map/reduce_scatter | solution.py:325
  702.4 305.2 %all-reduce.17.cloned.1.call-start = ((), (), s32[]{:S(2)}) async-start(), calls=%async_computation.27 | async-start | bytes 11796480
  724.3 344.9 %reduce-scatter.37.cloned.1.call-start = ((), (), s32[]{:S(2)}) async-start(), calls=%async_computation.29 | async-start | bytes 1566720
  730.8 401.7 %reduce-scatter.33.cloned.1.call-start = ((), (), s32[]{:S(2)}) async-start(), calls=%async_computation.26 | async-start | bytes 884736
  737.6 451.8 %reduce-scatter.35.cloned.1.call-start = ((), (), s32[]{:S(2)}) async-start(), calls=%async_computation.28 | async-start | bytes 8460288
  1007.7 183.8 %copy-start.1 = (bf16[1000,1152]{1,0:T(8,128)(2,1)S(1)}, bf16[1000,1152]{1,0:T(8,128)(2,1)}, u32[]{:S(2)}) copy-start(bf16[1000,1152]{1,0:T(8,128)(2,1)} %param.18) | copy-start | bytes 6912004
  (39 other events, 242.6 us)
Sparse Core Ops, SparseCore 0:
  10.2 75.0 all-gather.9
  87.5 50.3 all-gather.13
  140.1 34.5 all-gather.11
  176.6 39.1 all-gather.15
  221.3 33.5 reduce-scatter.18
  257.0 56.3 all-gather.19
  315.4 34.6 all-gather.17
  352.3 56.2 all-gather.21
  410.8 34.6 all-gather.23
  472.1 34.7 reduce-scatter.22
  509.1 34.7 reduce-scatter.20
  550.7 36.0 all-gather.25
  626.3 34.7 reduce-scatter.24
  679.9 28.3 reduce-scatter.30
  712.1 78.0 reduce-scatter.28
  794.1 77.0 reduce-scatter.26
  874.8 132.8 all-reduce.16
  1011.3 57.8 reduce-scatter.36
  1072.0 14.2 reduce-scatter.32
  1090.3 99.1 reduce-scatter.34
where the time goes:
time: 1210 us; the launch traced here: 1200 us
  waiting for transfers between devices  768 us (63%)
  matrix products  157 us (13%)
  blocking collectives  129 us (11%)
  other arithmetic  66.1 us (5%)
  local copies, waits for them, and re-layouts  56.7 us (5%)
  between operations  19.1 us (2%)
    unnamed x25, waiting for transfers between devices  253 us
    unnamed x2, blocking collectives  124 us
    reduce_scatter x1, waiting for transfers between devices, local(): lax.psum_scatter(up_weight_grad.astype(jnp.bfloat16), 'col', scatter_dime...  79.2 us
    all_gather x1, waiting for transfers between devices, local(): lax.all_gather(up_weight, 'col', axis=0, tiled=True)  47 us
    all_gather x1, waiting for transfers between devices, local(): lax.all_gather(down_weight, 'col', axis=1, tiled=True)  47 us
    reduce_scatter x1, waiting for transfers between devices, local(): lax.psum_scatter(down_weight_grad.astype(jnp.bfloat16), 'col', scatter_di...  40.8 us
    all_gather x1, waiting for transfers between devices, local(): flat_mlp = lax.all_gather(grad_mlp, 'row', axis=0, tiled=True)  36.8 us
    all_gather x1, waiting for transfers between devices, local(): flat_two = lax.all_gather(hidden_two, 'row', axis=0, tiled=True)  36.8 us
  transfers between devices with their start and end apart: 20, of which 17 were waited for; matrix products, arithmetic and copies ran while one was open for 14% of the time, Pallas kernels for 0%

commit v1 on v0

--- a/solution.py
+++ b/solution.py
@@ -339,37 +339,309 @@
     return (block_out, tokens_grad, cond_grad) + summed_grads
 
 
+PAIR = ((0, 1), (1, 0))
+ALL = ("row", "chip", "core")
+COL = ("chip", "core")
+
+
+def exchange(values, axis="core"):
+    return lax.ppermute(values, axis, PAIR)
+
+
+def both(values):
+    return jnp.concatenate([values, exchange(values)], axis=0)
+
+
+def spread(block):
+    moved = lax.ppermute(block, ("row", "core"), ((0, 0), (1, 2), (2, 1), (3, 3)))
+    return lax.all_gather(moved, ("chip", "row"), axis=0, tiled=True)
+
+
+def collect(grad):
+    summed = lax.psum_scatter(
+        grad.astype(jnp.bfloat16), ("chip", "row"), scatter_dimension=0, tiled=True
+    )
+    return lax.ppermute(summed, ("row", "core"), ((0, 0), (1, 2), (2, 1), (3, 3))).astype(
+        jnp.float32
+    )
+
+
+def paired(
+    tokens,
+    labels,
+    timesteps,
+    class_table,
+    ada_weight,
+    ada_bias,
+    qkv_weight,
+    qkv_bias,
+    proj_weight,
+    proj_bias,
+    up_weight,
+    up_bias,
+    down_weight,
+    down_bias,
+    cotangent,
+):
+    f32 = jnp.float32
+    low = jnp.bfloat16
+    rows = tokens.shape[0]
+    mine = rows // SEQ
+    shared = labels.shape[0]
+    row = lax.axis_index("row")
+    core = lax.axis_index("core")
+    col = lax.axis_index(COL)
+    n_row = lax.axis_size("row")
+    n_col = lax.axis_size(COL)
+    latents = shared * n_col
+    k_rows, mod_half = ada_weight.shape
+
+    small = (ada_bias, qkv_bias, up_bias, proj_bias, down_bias, labels, timesteps)
+    packed = jnp.concatenate([v.astype(f32) for v in small])
+    used = packed.shape[0]
+    packed = jnp.pad(packed, (0, -used % 1024)).reshape(-1, 128)
+    fetched = lax.all_gather(packed, ALL, axis=0, tiled=False).reshape(n_row, n_col, -1)
+    pieces = []
+    start = 0
+    for v in small:
+        pieces.append(fetched[:, :, start : start + v.shape[0]])
+        start += v.shape[0]
+    ada_bias_full = pieces[0].reshape(-1)
+    qkv_bias_half = lax.dynamic_index_in_dim(pieces[1], core, 0, False).reshape(-1)
+    up_bias_half = lax.dynamic_index_in_dim(pieces[2], core, 0, False).reshape(-1)
+    proj_bias_full = pieces[3][0].reshape(-1)
+    down_bias_full = pieces[4][0].reshape(-1)
+    all_labels = pieces[5][0].reshape(-1).astype(jnp.int32)
+    all_steps = pieces[6][0].reshape(-1).astype(jnp.int32)
+
+    width = qkv_weight.shape[2]
+    heads = width // HD
+    qkv_full = spread(qkv_weight.transpose(1, 0, 2).reshape(k_rows, 3 * width))
+    proj_full = spread(proj_weight.T)
+    up_full = spread(up_weight)
+    down_full = spread(down_weight.T)
+
+    conditioning = condition(all_labels, all_steps, class_table)
+    activated = (conditioning * jax.nn.sigmoid(conditioning)).astype(low)
+    act_block = lax.dynamic_slice_in_dim(activated, col * k_rows, k_rows, 1)
+    mod_part = jnp.dot(act_block, ada_weight, preferred_element_type=f32)
+    mod_some = lax.psum_scatter(
+        mod_part.reshape(n_col, shared, mod_half), COL, scatter_dimension=0, tiled=False
+    )
+    mod_mine = lax.dynamic_slice_in_dim(mod_some, row * mine, mine, 0)
+    mod_theirs = lax.dynamic_slice_in_dim(mod_some, (1 - row) * mine, mine, 0)
+    mod_came = exchange(mod_theirs, "row")
+    modulation = (
+        jnp.concatenate(
+            [jnp.where(row == 0, mod_mine, mod_came), jnp.where(row == 0, mod_came, mod_mine)],
+            axis=1,
+        )
+        + ada_bias_full
+    )
+    parts = [modulation[:, None, block * D : (block + 1) * D] for block in range(6)]
+    shift_one, scale_one, gate_one, shift_two, scale_two, gate_two = parts
+
+    def tall(values):
+        return values.reshape(mine, SEQ, D)
+
+    def flat(values):
+        return values.reshape(rows, D)
+
+    upstream = tall(cotangent).astype(f32)
+    grad_mlp = flat((gate_two * upstream).astype(low))
+    flat_mlp = both(grad_mlp)
+
+    source = tall(tokens).astype(f32)
+    normed_one, inv_one = normalize(source)
+    hidden_one = flat((normed_one * (1.0 + scale_one) + shift_one).astype(low))
+    flat_one = both(hidden_one)
+    bias_pair = qkv_bias_half.reshape(heads, 2, HD)
+    bias_col = jnp.concatenate(
+        [bias_pair[:, 0].reshape(width), jnp.zeros((width,), f32), bias_pair[:, 1].reshape(width)]
+    ).reshape(3 * width, 1)
+    qkv_cols = (contract_cross(qkv_full, flat_one) + bias_col).astype(low)
+    query_cols = qkv_cols[:width]
+    key_cols = qkv_cols[width : 2 * width]
+    value_cols = qkv_cols[2 * width :]
+    attended, logsum = attend(query_cols, key_cols, value_cols, heads, shared)
+    there = exchange(contract_cross(attended[:, rows:], proj_full).astype(low))
+    here = contract_cross(attended[:, :rows], proj_full)
+    attn_out = tall(here + there.astype(f32) + proj_bias_full)
+    middle = source + gate_one * attn_out
+    normed_two, inv_two = normalize(middle)
+    hidden_two = flat((normed_two * (1.0 + scale_two) + shift_two).astype(low))
+    flat_two = both(hidden_two)
+    pre_act = jnp.dot(flat_two, up_full, preferred_element_type=f32) + up_bias_half
+    activ_full, slopes = gelu_pair(pre_act)
+    activ = activ_full.astype(low)
+    down_grad = collect(contract_rows(flat_mlp, activ)).T
+    grad_pre = (jnp.dot(flat_mlp, down_full, preferred_element_type=f32) * slopes).astype(low)
+    there = exchange(contract_cols(grad_pre[rows:], up_full).astype(low))
+    here = contract_cols(grad_pre[:rows], up_full)
+    grad_hidden_two = tall(here + there.astype(f32))
+    up_grad = collect(contract_rows(flat_two, grad_pre))
+    there = exchange(contract_cols(activ[rows:], down_full).astype(low))
+    here = contract_cols(activ[:rows], down_full)
+    mlp_out = tall(here + there.astype(f32) + down_bias_full)
+    block_out = flat((middle + gate_two * mlp_out).astype(low))
+
+    grad_middle = upstream + normalize_back(
+        normed_two, inv_two, grad_hidden_two * (1.0 + scale_two)
+    )
+    grad_attn = flat((gate_one * grad_middle).astype(low))
+    flat_grad_attn = both(grad_attn)
+    grad_attended = contract_cross(proj_full, flat_grad_attn).astype(low)
+    grads = jnp.concatenate(
+        attend_back(query_cols, key_cols, value_cols, logsum, grad_attended, heads, shared), axis=0
+    )
+    there = exchange(contract_cross(grads[:, rows:], qkv_full).astype(low))
+    here = contract_cross(grads[:, :rows], qkv_full)
+    grad_hidden_one = tall(here + there.astype(f32))
+    proj_grad = collect(contract_cross(flat_grad_attn, attended)).T
+    qkv_grad = (
+        collect(contract_cross(flat_one, grads)).reshape(k_rows, 3, width).transpose(1, 0, 2)
+    )
+    tokens_grad = flat(
+        grad_middle
+        + normalize_back(normed_one, inv_one, grad_hidden_one * (1.0 + scale_one))
+    )
+
+    grad_mod = jnp.concatenate(
+        [
+            jnp.sum(term, axis=1)
+            for term in (
+                grad_hidden_one,
+                grad_hidden_one * normed_one,
+                grad_middle * attn_out,
+                grad_hidden_two,
+                grad_hidden_two * normed_two,
+                upstream * mlp_out,
+            )
+        ],
+        axis=1,
+    ).astype(low)
+    mod_all = lax.all_gather(grad_mod, COL + ("row",), axis=0, tiled=False)
+    mod_all = lax.dynamic_slice_in_dim(mod_all, row * mod_half, mod_half, 2).reshape(
+        latents, mod_half
+    )
+    ada_bias_sum = jnp.sum(mod_all, axis=0, dtype=f32)
+    ada_bias_grad = lax.dynamic_slice_in_dim(
+        ada_bias_sum, col * ada_bias.shape[0], ada_bias.shape[0], 0
+    )
+    ada_weight_grad = contract_rows(act_block, mod_all)
+    act_part = contract_cols(mod_all, ada_weight)
+    act_all = lax.all_gather(act_part, ALL, axis=0, tiled=False).reshape(
+        n_row, n_col, latents, k_rows
+    )
+    slice_blocks = n_col // n_row
+    act_mine = lax.dynamic_slice(
+        act_all,
+        (0, row * slice_blocks, col * shared, 0),
+        (n_row, slice_blocks, shared, k_rows),
+    )
+    grad_activated = (
+        jnp.sum(act_mine, axis=0).transpose(1, 0, 2).reshape(shared, slice_blocks * k_rows)
+    )
+    cond_slice = lax.dynamic_slice(
+        conditioning,
+        (col * shared, row * slice_blocks * k_rows),
+        (shared, slice_blocks * k_rows),
+    )
+    sigmoid_slice = jax.nn.sigmoid(cond_slice)
+    cond_grad = grad_activated * sigmoid_slice * (1.0 + cond_slice * (1.0 - sigmoid_slice))
+
+    sums = jnp.sum(grads, axis=1, dtype=f32)
+    qkv_bias_sum = jnp.stack(
+        [sums[:width].reshape(heads, HD), sums[2 * width :].reshape(heads, HD)], axis=1
+    )
+    up_bias_sum = jnp.sum(grad_pre, axis=0, dtype=f32)
+    proj_bias_sum = jnp.sum(grad_attn, axis=0, dtype=f32)
+    down_bias_sum = jnp.sum(grad_mlp, axis=0, dtype=f32)
+    is_half = (jnp.arange(n_row) == core).astype(f32)[:, None, None]
+
+    def halved(values):
+        return is_half * values.reshape(1, n_col, -1)
+
+    def repeated(values):
+        return jnp.broadcast_to(values.reshape(1, n_col, -1), (n_row, n_col, values.size // n_col))
+
+    sums = jnp.concatenate(
+        [
+            halved(qkv_bias_sum),
+            halved(up_bias_sum),
+            repeated(proj_bias_sum),
+            repeated(down_bias_sum),
+        ],
+        axis=2,
+    )
+    sums = jnp.pad(sums, ((0, 0), (0, 0), (0, -sums.shape[2] % 1024)))
+    own = lax.psum_scatter(
+        sums.reshape(n_row * n_col, -1, 128), ALL, scatter_dimension=0, tiled=False
+    ).reshape(-1)
+    bias_grads = []
+    start = 0
+    for v in (qkv_bias, up_bias, proj_bias, down_bias):
+        bias_grads.append(own[start : start + v.shape[0]])
+        start += v.shape[0]
+    return (
+        block_out,
+        tokens_grad,
+        cond_grad,
+        ada_weight_grad,
+        ada_bias_grad,
+        qkv_grad,
+        bias_grads[0],
+        proj_grad,
+        bias_grads[2],
+        up_grad,
+        bias_grads[1],
+        down_grad,
+        bias_grads[3],
+    )
+
+
 def solution(mesh):
+    if mesh.shape["row"] == 2 and mesh.shape["col"] % 2 == 0:
+        split = jax.sharding.Mesh(
+            mesh.devices.reshape(2, mesh.shape["col"] // 2, 2), ("row", "chip", "core")
+        )
+        assert mesh.axis_names == ("row", "col")
+        return over(split, paired, COL)
+    return over(mesh, local, ("col",))
+
+
+def over(mesh, body, col):
+    row = ("row",)
     in_specs = (
-        P(("col", "row"), None),
-        P("col"),
-        P("col"),
+        P(col + row, None),
+        P(col),
+        P(col),
         P(),
-        P("col", "row"),
-        P(("row", "col")),
-        P(None, "col", "row"),
-        P(("row", "col")),
-        P("row", "col"),
-        P("col"),
-        P("col", "row"),
-        P(("row", "col")),
-        P("row", "col"),
-        P("col"),
-        P(("col", "row"), None),
+        P(col, "row"),
+        P(row + col),
+        P(None, col, "row"),
+        P(row + col),
+        P("row", col),
+        P(col),
+        P(col, "row"),
+        P(row + col),
+        P("row", col),
+        P(col),
+        P(col + row, None),
     )
     out_specs = (
-        P(("col", "row"), None),
-        P(("col", "row"), None),
-        P("col", "row"),
-        P("col", "row"),
-        P(("row", "col")),
-        P(None, "col", "row"),
-        P(("row", "col")),
-        P("row", "col"),
-        P("col"),
-        P("col", "row"),
-        P(("row", "col")),
-        P("row", "col"),
-        P("col"),
-    )
-    return jax.shard_map(local, mesh=mesh, in_specs=in_specs, out_specs=out_specs, check_vma=False)
+        P(col + row, None),
+        P(col + row, None),
+        P(col, "row"),
+        P(col, "row"),
+        P(row + col),
+        P(None, col, "row"),
+        P(row + col),
+        P("row", col),
+        P(col),
+        P(col, "row"),
+        P(row + col),
+        P("row", col),
+        P(col),
+    )
+    return jax.shard_map(body, mesh=mesh, in_specs=in_specs, out_specs=out_specs, check_vma=False)

time: 1210 us -> 1050 us (0.87)
  waiting for transfers between devices: 768 us -> 616 us
  blocking collectives: 129 us -> 157 us
  other arithmetic: 66.1 us -> 39.1 us
  starting transfers between devices: 2.06 us -> 28.6 us
  matrix products: 157 us -> 141 us
    all_gather x1 -> x3, blocking collectives: 4.81 us -> 157 us  [the longest x1 72 us: paired(): mod_all = lax.all_gather(grad_mod, COL + ('row',), axis=0, tiled=False)]
    all_gather x9 -> x4, waiting for transfers between devices: 273 us -> 125 us  [spread(): return lax.all_gather(moved, ('chip', 'row'), axis=0, tiled=True)]
    unnamed x2 -> x0, blocking collectives: 124 us -> none
    unnamed x25 -> x13, waiting for transfers between devices: 253 us -> 184 us
    reduce_scatter x6 -> x3, waiting for transfers between devices: 242 us -> 298 us  [collect(): lax.psum_scatter(grad.astype(jnp.bfloat16), ('chip', 'row'), scatter_dime...]
    ppermute x0 -> x17, starting transfers between devices: none -> 27.4 us  [the longest x4 14.3 us: collect(): lax.ppermute(summed, ('row', 'core'), ((0, 0), (1, 2), (2, 1), (3, 3)))]
    convert_element_type x18 -> x7, other arithmetic: 26 us -> 5.77 us  [the longest x1 1.86 us: collect(): lax.ppermute(summed, ('row', 'core'), ((0, 0), (1, 2), (2, 1), (3, 3)))]
    dot_general x9 -> x8, matrix products: 30.1 us -> 47.7 us  [contract_cross(): lax.dot_general(left, right, (((0,), (1,)), ((), ())), preferred_element_...]
  transfers between devices with their start and end apart: 20 -> 27, of which waited for: 17 -> 12; matrix products, arithmetic and copies ran while one was open for 14% -> 14% of each run, Pallas kernels for 0% -> 0%
where the time goes in v1:
time: 1050 us; the launch traced here: 1040 us
  waiting for transfers between devices  616 us (59%)
  blocking collectives  157 us (15%)
  matrix products  141 us (13%)
  local copies, waits for them, and re-layouts  44.7 us (4%)
  other arithmetic  39.1 us (4%)
  starting transfers between devices  28.6 us (3%)
  between operations  17.5 us (2%)
    reduce_scatter x3, waiting for transfers between devices, collect(): lax.psum_scatter(grad.astype(jnp.bfloat16), ('chip', 'row'), scatter_dime...  298 us
    unnamed x13, waiting for transfers between devices  184 us
    all_gather x4, waiting for transfers between devices, spread(): return lax.all_gather(moved, ('chip', 'row'), axis=0, tiled=True)  125 us
    all_gather x1, blocking collectives, paired(): mod_all = lax.all_gather(grad_mod, COL + ('row',), axis=0, tiled=False)  72 us
    dot_general x8, matrix products, contract_cross(): lax.dot_general(left, right, (((0,), (1,)), ((), ())), preferred_element_...  47.7 us
    all_gather x1, blocking collectives, paired(): lax.all_gather(packed, ALL, axis=0, tiled=False).reshape(n_row, n_col, -1)  43.6 us
    all_gather x1, blocking collectives, paired(): lax.all_gather(act_part, ALL, axis=0, tiled=False)  41.3 us
    dot_general x5, matrix products, contract_cols(): lax.dot_general(left, right, (((1,), (1,)), ((), ())), preferred_element_...  28 us
  transfers between devices with their start and end apart: 27, of which 12 were waited for; matrix products, arithmetic and copies ran while one was open for 14% of the time, Pallas kernels for 0%

profile of v1, /device:TPU:0, one launch (start us, length us, event | category | flops | bytes accessed | tf_op | source)
XLA Modules:
  0.0 1043.9 jit_solution(18204063040225365988)
XLA Ops:
  13.0 43.6 %all_gather.25 = f32[32,8,128]{2,1,0:T(8,128)S(1)} all-gather(f32[1,8,128]{2,1,0:T(8,128)S(1)} %pad_bitcast_fusion), channel_id=1, replica_groups=mesh['row'=2,'chip'=8,'core'=2] {'row','chip','core'}, dimensions={0}, use_global_device_ids=true | all-gather | bytes 135168 | tf_op jit(solution)/shard_map/all_gather | solution.py:403
  67.7 103.2 %all-reduce.8.cloned.1.call-done = f32[16,4,3456]{2,1,0:T(4,128)} async-done(((f32[16,4,3456]{2,1,0:T(4,128)}), f32[16,4,3456]{2,1,0:T(4,128)}) %all-reduce.8.cloned.1.call-update) | async-done | bytes 884752
  180.4 7.3 fusion.25
  216.6 7.3 collective-permute-start.4
  236.4 51.9 %all-gather.10.cloned.1.call-done = bf16[1152,2304]{1,0:T(8,128)(2,1)} async-done(((bf16[72,2304]{1,0:T(8,128)(2,1)}), bf16[1152,2304]{1,0:T(8,128)(2,1)}) %all-gather.10.cloned.1.call-update) | async-done | bytes 5308432 | tf_op jit(solution)/shard_map/all_gather | solution.py:357
  288.3 14.2 %multiply_convert_fusion = (bf16[1024,2304]{1,0:T(8,128)(2,1)}, f32[1024,2304]{1,0:T(8,128)}) fusion(f32[2304]{0:T(1024)S(1)} %add.250, bf16[1152,2304]{1,0:T(8,128)(2,1)} %all-gather.10.cloned.1.call-done, bf16[512,1152]{1,0:T(8,128)(2,1)} %collective-permute-done.5, bf16[512,1152]{1,0:T(8,128)(2,1)} %fusion.34), kind=kOutput, calls=%fused_computation.13 | convolution fusion | flops 5464129536 | bytes 21832704 | tf_op jit(solution)/shard_map/dot_general | solution.py:474
  302.4 72.8 %all-gather.12.cloned.1.call-done = bf16[1152,2304]{1,0:T(8,128)(2,1)} async-done(((bf16[72,2304]{1,0:T(8,128)(2,1)}), bf16[1152,2304]{1,0:T(8,128)(2,1)}) %all-gather.12.cloned.1.call-update) | async-done | bytes 5308432 | tf_op jit(solution)/shard_map/all_gather | solution.py:357
  375.2 14.5 %convert_reduce_fusion = (f32[2304]{0:T(1024)S(1)}, bf16[1024,2304]{1,0:T(8,128)(2,1)S(1)}) fusion(f32[1024,2304]{1,0:T(8,128)} %get-tuple-element.92, f32[2304]{0:T(1024)S(1)} %add.250, bf16[1152,2304]{1,0:T(8,128)(2,1)} %all-gather.12.cloned.1.call-done, bf16[512,1152]{1,0:T(8,128)(2,1)} %collective-permute-done.9, bf16[512,1152]{1,0:T(8,128)(2,1)} %get-tuple-element.57), kind=kOutput, calls=%fused_computation.12 | convolution fusion | flops 5492439040 | bytes 21841920 | tf_op jit(solution)/shard_map/dot_general | solution.py:478
  400.2 7.8 fusion.42
  408.1 11.4 %convert_reduce_fusion.3 = (f32[1152]{0:T(1024)S(1)}, bf16[512,1152]{1,0:T(8,128)(2,1)}, f32[512,1152]{1,0:T(8,128)}, bf16[512,1152]{1,0:T(8,128)(2,1)}, f32[512,1152]{1,0:T(8,128)}) fusion(f32[2,1152]{1,0:T(2,128)S(1)} %get-tuple-element.79, f32[512]{0:T(512)S(1)} %get-tuple-element.97, f32[512,1152]{1,0:T(8,128)S(1)} %copy-done.4, ...), kind=kOutput, calls=%fused_computation.81 | convolution fusion | flops 2729114624 | bytes 21868544 | tf_op jit(solution)/shard_map/dot_general | solution.py:61
  422.8 4.8 fusion.70
  434.2 9.3 multiply_convert_fusion.1
  457.4 5.2 convolution_convert_fusion.3
  463.0 9.2 convolution_convert_fusion.2
  472.3 10.5 %convolution_convert_fusion.1 = bf16[1152,2304]{1,0:T(8,128)(2,1)} fusion(bf16[1024,2304]{1,0:T(8,128)(2,1)} %copy-done.26, bf16[512,1152]{1,0:T(8,128)(2,1)} %collective-permute-done.5, bf16[512,1152]{1,0:T(8,128)(2,1)} %fusion.34), kind=kOutput, calls=%fused_computation.4 | convolution fusion | flops 5443190784 | bytes 12386304 | tf_op jit(solution)/shard_map/dot_general | solution.py:55
  483.1 10.6 %convolution_convert_fusion = bf16[1152,2304]{1,0:T(8,128)(2,1)} fusion(bf16[1024,2304]{1,0:T(8,128)(2,1)} %get-tuple-element.91, bf16[512,1152]{1,0:T(8,128)(2,1)} %collective-permute-done.9, bf16[512,1152]{1,0:T(8,128)(2,1)} %get-tuple-element.57), kind=kOutput, calls=%fused_computation.3 | convolution fusion | flops 5443190784 | bytes 12386304 | tf_op jit(solution)/shard_map/dot_general | solution.py:55
  493.7 6.4 convolution_convert_fusion.4
  500.6 80.5 %all-reduce.10.cloned.1.call-done = f32[32,8,128]{2,1,0:T(8,128)} async-done(((f32[32,8,128]{2,1,0:T(8,128)}), f32[32,8,128]{2,1,0:T(8,128)}) %all-reduce.10.cloned.1.call-update) | async-done | bytes 131088
  583.0 6.4 fusion.41
  592.8 72.0 %all_gather.30 = bf16[32,2,6912]{2,1,0:T(2,128)(2,1)S(1)} all-gather(bf16[1,2,6912]{2,1,0:T(2,128)(2,1)S(1)} %constant_dynamic-update-slice_fusion.3), channel_id=1, replica_groups=mesh['row'=2,'chip'=8,'core'=2] {'chip','core','row'}, dimensions={0}, use_global_device_ids=true | all-gather | bytes 912384 | tf_op jit(solution)/shard_map/all_gather | solution.py:523
  665.7 41.3 %all-gather = f32[2048,72]{1,0:T(8,128)S(1)} all-gather(f32[64,72]{1,0:T(8,128)S(1)} %fusion.105), channel_id=2, replica_groups=mesh['row'=2,'chip'=8,'core'=2] {'row','chip','core'}, dimensions={0}, use_global_device_ids=true | all-gather | bytes 608256 | tf_op jit(solution)/shard_map/all_gather | solution.py:533
  712.9 13.3 %reduce-scatter.7.cloned.1.call-done = bf16[72,1728]{1,0:T(8,128)(2,1)} async-done(((bf16[1152,1728]{1,0:T(8,128)(2,1)}), bf16[72,1728]{1,0:T(8,128)(2,1)}) %reduce-scatter.7.cloned.1.call-update) | async-done | bytes 248848 | tf_op jit(solution)/shard_map/reduce_scatter | solution.py:361
  729.8 143.0 %reduce-scatter.9.cloned.1.call-done = bf16[72,2304]{1,0:T(8,128)(2,1)} async-done(((bf16[1152,2304]{1,0:T(8,128)(2,1)}), bf16[72,2304]{1,0:T(8,128)(2,1)}) %reduce-scatter.9.cloned.1.call-update) | async-done | bytes 331792 | tf_op jit(solution)/shard_map/reduce_scatter | solution.py:361
  877.0 142.2 %reduce-scatter.11.cloned.1.call-done = bf16[72,2304]{1,0:T(8,128)(2,1)} async-done(((bf16[1152,2304]{1,0:T(8,128)(2,1)}), bf16[72,2304]{1,0:T(8,128)(2,1)}) %reduce-scatter.11.cloned.1.call-update) | async-done | bytes 331792 | tf_op jit(solution)/shard_map/reduce_scatter | solution.py:361
  (272 shorter events, 137.8 us)
Async XLA Ops:
  8.0 162.9 %all-reduce.8.cloned.1.call-start = ((), (), s32[]{:S(2)}) async-start(), calls=%async_computation.11 | async-start | bytes 1769472
  60.9 119.5 %all-gather.6.cloned.1.call-start = ((), (), s32[]{:S(2)}) async-start(), calls=%async_computation.4 | async-start | bytes 4386816 | tf_op jit(solution)/shard_map/all_gather | solution.py:357
  62.8 149.9 %all-gather.8.cloned.1.call-start = ((), (), s32[]{:S(2)}) async-start(), calls=%async_computation.5 | async-start | bytes 1566720 | tf_op jit(solution)/shard_map/all_gather | solution.py:357
  64.2 224.1 %all-gather.10.cloned.1.call-start = ((), (), s32[]{:S(2)}) async-start(), calls=%async_computation.6 | async-start | bytes 5640192 | tf_op jit(solution)/shard_map/all_gather | solution.py:357
  64.2 0.7 collective-permute-start.6
  65.7 309.6 %all-gather.12.cloned.1.call-start = ((), (), s32[]{:S(2)}) async-start(), calls=%async_computation.7 | async-start | bytes 5640192 | tf_op jit(solution)/shard_map/all_gather | solution.py:357
  171.7 3.9 collective-permute-start
  177.3 3.0 collective-permute-start.1
  178.8 402.2 %all-reduce.10.cloned.1.call-start = ((), (), s32[]{:S(2)}) async-start(), calls=%async_computation.12 | async-start | bytes 262144
  216.6 10.1 collective-permute-start.4
  233.2 3.2 collective-permute-start.5
  235.0 67.4 %collective-permute-start.9 = (bf16[512,1152]{1,0:T(8,128)(2,1)}, bf16[512,1152]{1,0:T(8,128)(2,1)}, u32[]{:S(2)}, u32[]{:S(2)}) collective-permute-start(bf16[512,1152]{1,0:T(8,128)(2,1)} %get-tuple-element.57), channel_id=1, source_target_pairs={{0,1},{1,0},{2,3},{3,2},{4,5},{5,4},{6,7},{7,6},{8,9},{9,8},{10,11... | collective-permute-start | bytes 3538952 | tf_op jit(solution)/shard_map/ppermute | solution.py:348
  394.0 6.1 collective-permute-start.10
  400.1 8.0 collective-permute-start.8
  419.5 3.3 collective-permute-start.11
  457.3 253.5 %reduce-scatter.13.cloned.1.call-start = ((), (), s32[]{:S(2)}) async-start(), calls=%async_computation.13 | async-start | bytes 1566720
  462.6 263.6 %reduce-scatter.7.cloned.1.call-start = ((), (), s32[]{:S(2)}) async-start(), calls=%async_computation.8 | async-start | bytes 4386816 | tf_op jit(solution)/shard_map/reduce_scatter | solution.py:361
  472.3 400.5 %reduce-scatter.9.cloned.1.call-start = ((), (), s32[]{:S(2)}) async-start(), calls=%async_computation.9 | async-start | bytes 5640192 | tf_op jit(solution)/shard_map/reduce_scatter | solution.py:361
  482.8 536.4 %reduce-scatter.11.cloned.1.call-start = ((), (), s32[]{:S(2)}) async-start(), calls=%async_computation.10 | async-start | bytes 5640192 | tf_op jit(solution)/shard_map/reduce_scatter | solution.py:361
  500.1 82.9 %collective-permute-start.12 = (bf16[512,1152]{1,0:T(8,128)(2,1)}, bf16[512,1152]{1,0:T(8,128)(2,1)}, u32[]{:S(2)}, u32[]{:S(2)}) collective-permute-start(bf16[512,1152]{1,0:T(8,128)(2,1)} %convolution_convert_fusion.4), channel_id=1, source_target_pairs={{0,1},{1,0},{2,3},{3,2},{4,5},{5,4},{6,7},{7,6},{8,9},{9,8},{10,11... | collective-permute-start | bytes 3538952 | tf_op jit(solution)/shard_map/ppermute | solution.py:348
  710.8 318.1 %collective-permute-start.14 = (bf16[72,576]{1,0:T(8,128)(2,1)}, bf16[72,576]{1,0:T(8,128)(2,1)}, u32[]{:S(2)}, u32[]{:S(2)}) collective-permute-start(bf16[72,576]{1,0:T(8,128)(2,1)} %reduce-scatter.13.cloned.1.call-done), channel_id=1, source_target_pairs={{0,0},{1,16},{16,1},{17,17},{2,2},{3,18},{18,3},{19,19},{4,4},{5,2... | collective-permute-start | bytes 248840 | tf_op jit(solution)/shard_map/ppermute | solution.py:364
  726.2 304.3 %collective-permute-start.13 = (bf16[72,1728]{1,0:T(8,128)(2,1)}, bf16[72,1728]{1,0:T(8,128)(2,1)}, u32[]{:S(2)}, u32[]{:S(2)}) collective-permute-start(bf16[72,1728]{1,0:T(8,128)(2,1)} %reduce-scatter.7.cloned.1.call-done), channel_id=1, source_target_pairs={{0,0},{1,16},{16,1},{17,17},{2,2},{3,18},{18,3},{19,19},{4,4},{5,2... | collective-permute-start | bytes 746504 | tf_op jit(solution)/shard_map/ppermute | solution.py:364
  872.7 159.8 %collective-permute-start.15 = (bf16[72,2304]{1,0:T(8,128)(2,1)}, bf16[72,2304]{1,0:T(8,128)(2,1)}, u32[]{:S(2)}, u32[]{:S(2)}) collective-permute-start(bf16[72,2304]{1,0:T(8,128)(2,1)} %reduce-scatter.9.cloned.1.call-done), channel_id=1, source_target_pairs={{0,0},{1,16},{16,1},{17,17},{2,2},{3,18},{18,3},{19,19},{4,4},{5,2... | collective-permute-start | bytes 995336 | tf_op jit(solution)/shard_map/ppermute | solution.py:364
  1019.2 15.2 %collective-permute-start.16 = (bf16[72,2304]{1,0:T(8,128)(2,1)}, bf16[72,2304]{1,0:T(8,128)(2,1)}, u32[]{:S(2)}, u32[]{:S(2)}) collective-permute-start(bf16[72,2304]{1,0:T(8,128)(2,1)} %reduce-scatter.11.cloned.1.call-done), channel_id=1, source_target_pairs={{0,0},{1,16},{16,1},{17,17},{2,2},{3,18},{18,3},{19,19},{4,4},{5,2... | collective-permute-start | bytes 995336 | tf_op jit(solution)/shard_map/ppermute | solution.py:364
  (50 other events, 936.2 us)
Sparse Core Ops, SparseCore 0:
  61.0 109.8 all-reduce.7
  457.5 123.5 all-reduce.9
Sparse Core Ops, SparseCore 1:
  64.7 77.7 all-gather.5
  145.1 56.7 all-gather.7
  205.1 83.2 all-gather.9
  291.7 83.5 all-gather.11
  463.0 117.9 reduce-scatter.12
  586.2 140.0 reduce-scatter.6
  731.3 141.3 reduce-scatter.8
  877.9 141.3 reduce-scatter.10
